TPU v7x, 32 devices: a whole 2x2x4 slice. The times are simulated.
32 devices in a mesh: row: 4 (over y, core), col: 8 (over z, x).
Axes of the slice: x: 2, y: 2, z: 4, core: 2. Of those that a mesh axis runs over, the one named last changes fastest.
Arguments:
- points: bfloat16 [65536, 512], P(('row', 'col')), may hold values from -6 to 6
- factor: bfloat16 [65536, 2048], P(('row', 'col')), may hold values from -0.078125 to 0.078125
- targets: bfloat16 [65536, 256], P(('row', 'col')), may hold values from -6 to 6
- pivot_slots: int32 [32, 32], P(('row', 'col')), may hold values from 0 to 2047, as said below
- pivot_counts: int32 [32], replicated, may hold values from 1 to 32, 512 in all
Outputs:
- new_columns: bfloat16 [512, 65536], P(None, ('row', 'col'))
- residual_next: float32 [65536, 256], P(('row', 'col'))
Inputs may be any that keep to these rules, and one draw needn't show every extreme that they name: `pivot_slots`: each row holds 32 different local row numbers; row d's first pivot_counts[d] entries are device d's pivots, the rest are unused. `pivot_counts`: the counts sum to 512; one of them is 32.
All inputs are finite; a program needn't handle non-finite values.
Results may differ from a plain program's by a relative error of at most 0.0029.
Values may be sent and summed in bfloat16 or wider, within the bound.
No kernel may reach another device: no remote copies, remote signals or barrier semaphores. Data moves between devices by JAX's collectives and lax.ppermute only.
A program may use at most 128 MiB of HBM per device.

v0:
```python
import jax
import jax.numpy as jnp
from jax import lax
from jax.sharding import PartitionSpec as P

BLOCK = 512
sharpness = 1.0
ridge_shift = 0.01
damping = 1.0
epsilon = 1e-06


def normalize(points):
    values = points.astype(jnp.float32)
    factor_scale = lax.rsqrt(jnp.mean(values * values, axis=1, keepdims=True) + epsilon)
    return (values * factor_scale).astype(jnp.bfloat16)


def kernel(left_rows, right_rows, feature_width):
    cosine = (
        lax.dot_general(
            left_rows, right_rows, (((1,), (1,)), ((), ())), preferred_element_type=jnp.float32
        )
        / feature_width
    )
    return jnp.exp(sharpness * (cosine - 1.0))


def compact_index(pivot_counts, block_size):
    owners_count = pivot_counts.shape[0]
    run_ends = jnp.cumsum(pivot_counts)
    run_starts = run_ends - pivot_counts
    position = jnp.arange(block_size, dtype=jnp.int32)
    owners = jnp.sum((position[:, None] >= run_ends[None, :]).astype(jnp.int32), axis=1)
    onehot = (owners[:, None] == jnp.arange(owners_count, dtype=jnp.int32)[None, :]).astype(
        jnp.int32
    )
    first_row = jnp.sum(onehot * run_starts[None, :], axis=1)
    return (owners, position - first_row)


def block_factor(pivot_scaled, pivot_factor):
    intersection = lax.dot_general(
        pivot_factor, pivot_factor, (((1,), (1,)), ((), ())), preferred_element_type=jnp.float32
    )
    diag_shift = ridge_shift + jnp.max(jnp.sum(jnp.abs(intersection), axis=1))
    ridged = (
        kernel(pivot_scaled, pivot_scaled, pivot_scaled.shape[1])
        - intersection
        + diag_shift * jnp.eye(intersection.shape[0], dtype=jnp.float32)
    )
    return jnp.linalg.cholesky(ridged)


def on_device(points, factor, targets, pivot_slots, pivot_counts):
    scaled = normalize(points)
    local_slots = pivot_slots[0]
    slot_cap = pivot_slots.shape[1]
    own_scaled = jnp.take(scaled, local_slots, axis=0)
    own_factor = jnp.take(factor, local_slots, axis=0)
    inner_scaled, inner_factor = (
        lax.all_gather(own_scaled, "col", axis=0, tiled=True),
        lax.all_gather(own_factor, "col", axis=0, tiled=True),
    )
    padded_scaled, padded_factor = (
        lax.all_gather(inner_scaled, "row", axis=0, tiled=True),
        lax.all_gather(inner_factor, "row", axis=0, tiled=True),
    )
    owners, slot_index = compact_index(pivot_counts, BLOCK)
    row_index = owners * slot_cap + slot_index
    pivot_scaled = jnp.take(padded_scaled, row_index, axis=0)
    pivot_factor = jnp.take(padded_factor, row_index, axis=0)
    lower_factor = block_factor(pivot_scaled, pivot_factor)
    downdated = kernel(pivot_scaled, scaled, scaled.shape[1]) - lax.dot_general(
        pivot_factor, factor, (((1,), (1,)), ((), ())), preferred_element_type=jnp.float32
    )
    new_columns = lax.linalg.triangular_solve(
        lower_factor, downdated, left_side=True, lower=True
    ).astype(jnp.bfloat16)
    cross_terms = jnp.concatenate(
        [
            lax.dot_general(
                factor, targets, (((0,), (0,)), ((), ())), preferred_element_type=jnp.float32
            ),
            lax.dot_general(
                new_columns, targets, (((1,), (0,)), ((), ())), preferred_element_type=jnp.float32
            ),
        ],
        axis=0,
    )
    col_norms = jnp.concatenate(
        [
            jnp.sum(jnp.square(factor.astype(jnp.float32)), axis=0),
            jnp.sum(jnp.square(new_columns.astype(jnp.float32)), axis=1),
        ],
        axis=0,
    )
    cross_whole, norm_whole = lax.psum((cross_terms, col_norms), ("row", "col"))
    coefficients = (cross_whole / (norm_whole + damping)[:, None]).astype(jnp.bfloat16)
    held_count = factor.shape[1]
    fitted = jnp.dot(factor, coefficients[:held_count], preferred_element_type=jnp.float32)
    fitted = fitted + lax.dot_general(
        new_columns,
        coefficients[held_count:],
        (((0,), (0,)), ((), ())),
        preferred_element_type=jnp.float32,
    )
    residual_next = targets.astype(jnp.float32) - fitted
    return (new_columns, residual_next)


def solution(mesh):
    return jax.shard_map(
        on_device,
        mesh=mesh,
        in_specs=(
            P(("row", "col"), None),
            P(("row", "col"), None),
            P(("row", "col"), None),
            P(("row", "col"), None),
            P(),
        ),
        out_specs=(P(None, ("row", "col")), P(("row", "col"), None)),
        check_vma=False,
    )
```

profile of v0, /device:TPU:0, one launch (start us, length us, event | category | flops | bytes accessed | tf_op | source)
XLA Modules:
  0.0 457.6 jit_solution(8331831617520132772)
XLA Ops:
  8.5 5.2 %gather_fusion.2 = bf16[32,2048]{1,0:T(8,128)(2,1)S(1)} fusion(bf16[2048,2048]{1,0:T(8,128)(2,1)} %param.6, s32[1024]{0:T(1024)S(1)} %pad_clamp_fusion.1), kind=kCustom, calls=%fused_computation.2 | custom fusion | bytes 262272 | tf_op jit(solution)/shard_map/jit(_take)/gather | solution.py:60
  14.6 2.2 fusion
  18.0 35.1 %all_gather.12 = bf16[256,512]{1,0:T(8,128)(2,1)} all-gather(bf16[32,512]{1,0:T(8,128)(2,1)S(1)} %broadcast_select_fusion.7), channel_id=1, replica_groups=mesh['row'=4,'col'=8] {'col'}, dimensions={0}, use_global_device_ids=true | all-gather | bytes 294912 | tf_op jit(solution)/shard_map/all_gather | solution.py:62
  53.2 5.6 %all-gather.6.cloned.1.call-done = bf16[256,2048]{1,0:T(8,128)(2,1)} async-done(((bf16[32,2048]{1,0:T(8,128)(2,1)}), bf16[256,2048]{1,0:T(8,128)(2,1)}) %all-gather.6.cloned.1.call-update) | async-done | bytes 1048592 | tf_op jit(solution)/shard_map/all_gather | solution.py:63
  59.5 7.2 %fusion.51 = f32[2048,256]{1,0:T(8,128)} fusion(bf16[2048,2048]{1,0:T(8,128)(2,1)} %param.6, bf16[2048,256]{1,0:T(8,128)(2,1)S(1)} %copy-done.6), kind=kOutput, calls=%fused_computation.122 | convolution fusion | flops 2147483648 | bytes 11534336 | tf_op jit(solution)/shard_map/dot_general | solution.py:82
  66.7 9.0 %all-gather.4.cloned.1.call-done = bf16[1024,512]{1,0:T(8,128)(2,1)} async-done(((bf16[256,512]{1,0:T(8,128)(2,1)}), bf16[1024,512]{1,0:T(8,128)(2,1)}) %all-gather.4.cloned.1.call-update) | async-done | bytes 1048592 | tf_op jit(solution)/shard_map/all_gather | solution.py:66
  75.7 4.0 gather_fusion.1
  79.7 32.0 %all-gather.8.cloned.1.call-done = bf16[1024,2048]{1,0:T(8,128)(2,1)} async-done(((bf16[256,2048]{1,0:T(8,128)(2,1)}), bf16[1024,2048]{1,0:T(8,128)(2,1)}) %all-gather.8.cloned.1.call-update) | async-done | bytes 4194320 | tf_op jit(solution)/shard_map/all_gather | solution.py:67
  111.8 8.0 %gather_fusion.3 = bf16[512,2048]{1,0:T(8,128)(2,1)} fusion(bf16[1024,2048]{1,0:T(8,128)(2,1)} %all-gather.8.cloned.1.call-done, s32[1024]{0:T(1024)S(1)} %pad_clamp_fusion), kind=kCustom, calls=%fused_computation.3 | custom fusion | bytes 4196352 | tf_op jit(solution)/shard_map/jit(_take)/gather | solution.py:72
  119.7 3.7 abs_reduce_fusion
  123.5 9.9 %fusion.21 = f32[512,2048]{1,0:T(8,128)} fusion(bf16[2048,2048]{1,0:T(8,128)(2,1)} %param.6, bf16[512,2048]{1,0:T(8,128)(2,1)S(1)} %copy-done.4, pred[512]{0:T(512)(128)(4,1)S(1)} %compare_and_fusion.1), kind=kOutput, calls=%fused_computation.51 | convolution fusion | flops 4296015872 | bytes 14680576 | tf_op jit(solution)/shard_map/dot_general | solution.py:74
  133.3 1.3 copy.20
  134.6 2.1 fusion.17
  136.8 1.3 copy.21
  139.3 1.4 add_multiply_fusion
  141.8 11.7 %cholesky.103 = f32[128,128]{1,0:T(8,128)S(1)} custom-call(f32[128,128]{1,0:T(8,128)S(1)} %cholesky.263), custom_call_target="Cholesky" | custom-call | tf_op jit(solution)/shard_map/jit(cholesky)/cholesky | solution.py:52
  153.7 9.8 %custom-call.30 = f32[1,128,128]{1,2,0:T(8,128)S(1)} custom-call(f32[1,128,128]{2,1,0:T(8,128)S(1)} %get-tuple-element.37), custom_call_target="InvertDiagBlocksLowerTriangular" | custom-call | tf_op jit(solution)/shard_map/jit(cholesky)/cholesky | solution.py:52
  163.5 1.2 constant_dynamic-update-slice_fusion.3
  164.7 1.3 convolution_subtract_fusion.2
  166.0 11.7 %cholesky.215 = f32[128,128]{1,0:T(8,128)S(1)} custom-call(f32[128,128]{1,0:T(8,128)S(1)} %cholesky.267), custom_call_target="Cholesky" | custom-call | tf_op jit(solution)/shard_map/jit(cholesky)/cholesky | solution.py:52
  177.8 10.2 %custom-call.31 = f32[1,128,128]{1,2,0:T(8,128)S(1)} custom-call(f32[1,128,128]{2,1,0:T(8,128)S(1)} %get-tuple-element.34), custom_call_target="InvertDiagBlocksLowerTriangular" | custom-call | tf_op jit(solution)/shard_map/jit(cholesky)/cholesky | solution.py:52
  188.3 1.3 convolution_subtract_fusion.3
  189.6 11.7 %cholesky.236 = f32[128,128]{1,0:T(8,128)S(1)} custom-call(f32[128,128]{1,0:T(8,128)S(1)} %cholesky.272), custom_call_target="Cholesky" | custom-call | tf_op jit(solution)/shard_map/jit(cholesky)/cholesky | solution.py:52
  202.0 9.8 %custom-call.32 = f32[1,128,128]{1,2,0:T(8,128)S(1)} custom-call(f32[1,128,128]{2,1,0:T(8,128)S(1)} %get-tuple-element.31), custom_call_target="InvertDiagBlocksLowerTriangular" | custom-call | tf_op jit(solution)/shard_map/jit(cholesky)/cholesky | solution.py:52
  212.0 1.2 convolution_subtract_fusion.4
  213.2 11.8 %cholesky.253 = f32[128,128]{1,0:T(8,128)S(1)} custom-call(f32[128,128]{1,0:T(8,128)S(1)} %convolution_subtract_fusion.4), custom_call_target="Cholesky" | custom-call | tf_op jit(solution)/shard_map/jit(cholesky)/cholesky | solution.py:52
  228.8 1.1 select_select_fusion
  229.9 13.6 %while.1 = (s32[]{:T(128)}, f32[512,512]{1,0:T(8,128)}, s32[4,2]{0,1:T(2,128)S(1)}, f32[4,128,128]{2,1,0:T(8,128)}, s32[]{:T(128)}) while((s32[]{:T(128)}, f32[512,512]{1,0:T(8,128)}, s32[4,2]{0,1:T(2,128)S(1)}, f32[4,128,128]{2,1,0:T(8,128)}, s32[]{:T(128)}) %tuple.39), condition=%wide.while_cond, body=%wide.while_body.sunk | while | flops 2 | bytes 132705 | solution.py:77
  230.6 2.8 bitcast_dynamic-update-slice_fusion.2
  234.0 2.8 bitcast_dynamic-update-slice_fusion.2
  237.4 2.8 bitcast_dynamic-update-slice_fusion.2
  240.8 2.7 bitcast_dynamic-update-slice_fusion.2
  243.6 40.1 %custom-call.33 = f32[4,128,128]{1,2,0:T(8,128)S(1)} custom-call(f32[4,128,128]{2,1,0:T(8,128)} %get-tuple-element.9), custom_call_target="InvertDiagBlocksLowerTriangular" | custom-call | tf_op jit(solution)/shard_map/triangular_solve | solution.py:77
  283.7 3.7 exponential_subtract_fusion
  287.4 1.1 fusion.50
  288.5 1.9 convolution_subtract_fusion.1
  291.4 2.2 convolution_subtract_fusion
  293.6 1.0 fusion.48
  294.7 3.0 fusion.9
  297.7 1.1 convolution_convert_fusion
  299.4 1.3 copy-done
  301.7 1.7 pad_maximum_fusion
  304.3 5.1 %multiply_reduce_fusion = f32[2048]{0:T(1024)S(1)} fusion(bf16[2048,2048]{1,0:T(8,128)(2,1)} %param.6), kind=kLoop, calls=%fused_computation.6 | loop fusion | flops 12580864 | bytes 8396800 | tf_op jit(solution)/shard_map/reduce_sum | solution.py:93
  309.4 39.6 %psum.15 = f32[2560]{0:T(1024)S(1)} all-reduce(f32[2560]{0:T(1024)S(1)} %pad_maximum_fusion.2), channel_id=1, replica_groups=mesh['row'=4,'col'=8] {'row','col'}, use_global_device_ids=true, to_apply=%region_17.18 | all-reduce | flops 2560 | bytes 20480 | tf_op jit(solution)/shard_map/psum | solution.py:98
  349.0 91.1 %all-reduce.3.cloned.1.call-done = f32[2560,256]{1,0:T(8,128)} async-done(((f32[2560,256]{1,0:T(8,128)}), f32[2560,256]{1,0:T(8,128)}) %all-reduce.3.cloned.1.call-update) | async-done | bytes 2621456 | tf_op jit(solution)/shard_map/psum | solution.py:98
  440.1 2.1 divide_convert_fusion
  442.3 5.9 %convolution_bitcast_fusion = f32[2048,256]{0,1:T(8,128)S(1)} fusion(bf16[2048,2048]{1,0:T(8,128)(2,1)} %param.6, bf16[2560,256]{1,0:T(8,128)(2,1)S(1)} %divide_convert_fusion), kind=kOutput, calls=%fused_computation.21 | convolution fusion | flops 2147483648 | bytes 11534336 | tf_op jit(solution)/shard_map/dot_general | solution.py:101
  449.0 1.8 copy.24
  (75 shorter events, 15.2 us)
Async XLA Ops:
  7.2 51.6 %all-gather.6.cloned.1.call-start = ((), (), s32[]{:S(2)}) async-start(), calls=%async_computation.1 | async-start | bytes 1179648 | tf_op jit(solution)/shard_map/all_gather | solution.py:63
  14.5 61.2 %all-gather.4.cloned.1.call-start = ((), (), s32[]{:S(2)}) async-start(), calls=%async_computation | async-start | bytes 1310720 | tf_op jit(solution)/shard_map/all_gather | solution.py:66
  14.6 2.3 copy-start.2
  16.8 42.1 %copy-start.8 = (s32[32]{0:T(128)S(1)}, s32[32]{0:T(128)}, u32[]{:S(2)}) copy-start(s32[32]{0:T(128)} %param.9) | copy-start | bytes 388
  16.9 42.7 %copy-start.6 = (bf16[2048,256]{1,0:T(8,128)(2,1)S(1)}, bf16[2048,256]{1,0:T(8,128)(2,1)}, u32[]{:S(2)}) copy-start(bf16[2048,256]{1,0:T(8,128)(2,1)} %param.7) | copy-start | bytes 3145732
  53.1 58.6 %all-gather.8.cloned.1.call-start = ((), (), s32[]{:S(2)}) async-start(), calls=%async_computation.2 | async-start | bytes 5242880 | tf_op jit(solution)/shard_map/all_gather | solution.py:67
  58.8 381.4 %all-reduce.3.cloned.1.call-start = ((), (), s32[]{:S(2)}) async-start(), calls=%async_computation.3 | async-start | bytes 5242880 | tf_op jit(solution)/shard_map/psum | solution.py:98
  119.7 3.8 copy-start.4
  140.8 1.0 copy-start.3
  297.7 3.0 copy-start.7
  299.4 1.3 copy-start
  299.4 2.3 copy-start.5
  442.3 5.9 %copy-start.1 = (bf16[512,2048]{1,0:T(8,128)(2,1)S(1)}, bf16[512,2048]{1,0:T(8,128)(2,1)}, u32[]{:S(2)}) copy-start(bf16[512,2048]{1,0:T(8,128)(2,1)} %copy-done) | copy-start | bytes 6291460
Sparse Core Ops, SparseCore 0:
  14.7 44.0 all-gather.5
  60.3 15.3 all-gather.3
  77.3 34.4 all-gather.7
  303.6 136.5 all-reduce.2
where the time goes:
time: 461 us; the launch traced here: 458 us
  waiting for transfers between devices  138 us (30%)
  other arithmetic  137 us (30%)
  blocking collectives  74.7 us (16%)
  matrix products  50.8 us (11%)
  local copies, waits for them, and re-layouts  39.5 us (9%)
  between operations  17.5 us (4%)
    psum x1, waiting for transfers between devices, on_device(): cross_whole, norm_whole = lax.psum((cross_terms, col_norms), ('row', 'col'))  91.1 us
    another operation x14, other arithmetic, block_factor(): return jnp.linalg.cholesky(ridged)  78.9 us
    another operation x3, other arithmetic, on_device(): lax.linalg.triangular_solve(lower_factor, downdated, left_side=True, lowe...  41.2 us
    psum x1, blocking collectives, on_device(): cross_whole, norm_whole = lax.psum((cross_terms, col_norms), ('row', 'col'))  39.6 us
    all_gather x1, blocking collectives, on_device(): lax.all_gather(own_scaled, 'col', axis=0, tiled=True)  35.1 us
    all_gather x1, waiting for transfers between devices, on_device(): lax.all_gather(inner_factor, 'row', axis=0, tiled=True)  32 us
    another operation x13, local copies, waits for them, and re-layouts  13.7 us
    another operation x7, matrix products, on_device(): lax.linalg.triangular_solve(lower_factor, downdated, left_side=True, lowe...  11.3 us
  transfers between devices with their start and end apart: 4, of which 4 were waited for; matrix products, arithmetic and copies ran while one was open for 5% of the time, Pallas kernels for 0%

commit v1 on v0

--- a/solution.py
+++ b/solution.py
@@ -95,7 +95,7 @@
         ],
         axis=0,
     )
-    cross_whole, norm_whole = lax.psum((cross_terms, col_norms), ("row", "col"))
+    cross_whole, norm_whole = lax.psum(lax.psum((cross_terms, col_norms), "col"), "row")
     coefficients = (cross_whole / (norm_whole + damping)[:, None]).astype(jnp.bfloat16)
     held_count = factor.shape[1]
     fitted = jnp.dot(factor, coefficients[:held_count], preferred_element_type=jnp.float32)

time: 461 us -> 502 us (1.089)
  waiting for transfers between devices: 138 us -> 172 us
  blocking collectives: 74.7 us -> 81.7 us
    psum x1 -> x2, waiting for transfers between devices: 91.1 us -> 125 us  [the longest x1 116 us: on_device(): lax.psum((cross_terms, col_norms), 'col')]
    psum x1 -> x2, blocking collectives: 39.6 us -> 46.7 us  [the longest x1 34.9 us: on_device(): lax.psum((cross_terms, col_norms), 'col')]
  transfers between devices with their start and end apart: 4 -> 5, of which waited for: 4 -> 5; matrix products, arithmetic and copies ran while one was open for 5% -> 4% of each run, Pallas kernels for 0% -> 0%
where the time goes in v1:
time: 502 us; the launch traced here: 499 us
  waiting for transfers between devices  172 us (34%)
  other arithmetic  137 us (27%)
  blocking collectives  81.7 us (16%)
  matrix products  50.8 us (10%)
  local copies, waits for them, and re-layouts  39.5 us (8%)
  between operations  17.5 us (3%)
    psum x1, waiting for transfers between devices, on_device(): lax.psum((cross_terms, col_norms), 'col')  116 us
    another operation x14, other arithmetic, block_factor(): return jnp.linalg.cholesky(ridged)  78.9 us
    another operation x3, other arithmetic, on_device(): lax.linalg.triangular_solve(lower_factor, downdated, left_side=True, lowe...  41.2 us
    all_gather x1, blocking collectives, on_device(): lax.all_gather(own_scaled, 'col', axis=0, tiled=True)  35.1 us
    psum x1, blocking collectives, on_device(): lax.psum((cross_terms, col_norms), 'col')  34.9 us
    all_gather x1, waiting for transfers between devices, on_device(): lax.all_gather(inner_factor, 'row', axis=0, tiled=True)  32 us
    another operation x13, local copies, waits for them, and re-layouts  13.7 us
    psum x1, blocking collectives, on_device(): lax.psum(lax.psum((cross_terms, col_norms), 'col'), 'row')  11.8 us
  transfers between devices with their start and end apart: 5, of which 5 were waited for; matrix products, arithmetic and copies ran while one was open for 4% of the time, Pallas kernels for 0%

profile of v1, /device:TPU:0, one launch (start us, length us, event | category | flops | bytes accessed | tf_op | source)
XLA Modules:
  0.0 498.5 jit_solution(2001025210053254846)
XLA Ops:
  8.5 5.2 %gather_fusion.2 = bf16[32,2048]{1,0:T(8,128)(2,1)S(1)} fusion(bf16[2048,2048]{1,0:T(8,128)(2,1)} %param.6, s32[1024]{0:T(1024)S(1)} %pad_clamp_fusion.1), kind=kCustom, calls=%fused_computation.2 | custom fusion | bytes 262272 | tf_op jit(solution)/shard_map/jit(_take)/gather | solution.py:60
  14.6 2.2 fusion
  18.0 35.1 %all_gather.12 = bf16[256,512]{1,0:T(8,128)(2,1)} all-gather(bf16[32,512]{1,0:T(8,128)(2,1)S(1)} %broadcast_select_fusion.7), channel_id=1, replica_groups=mesh['row'=4,'col'=8] {'col'}, dimensions={0}, use_global_device_ids=true | all-gather | bytes 294912 | tf_op jit(solution)/shard_map/all_gather | solution.py:62
  53.2 5.6 %all-gather.6.cloned.1.call-done = bf16[256,2048]{1,0:T(8,128)(2,1)} async-done(((bf16[32,2048]{1,0:T(8,128)(2,1)}), bf16[256,2048]{1,0:T(8,128)(2,1)}) %all-gather.6.cloned.1.call-update) | async-done | bytes 1048592 | tf_op jit(solution)/shard_map/all_gather | solution.py:63
  59.5 7.2 %fusion.51 = f32[2048,256]{1,0:T(8,128)} fusion(bf16[2048,2048]{1,0:T(8,128)(2,1)} %param.6, bf16[2048,256]{1,0:T(8,128)(2,1)S(1)} %copy-done.6), kind=kOutput, calls=%fused_computation.122 | convolution fusion | flops 2147483648 | bytes 11534336 | tf_op jit(solution)/shard_map/dot_general | solution.py:82
  66.7 9.0 %all-gather.4.cloned.1.call-done = bf16[1024,512]{1,0:T(8,128)(2,1)} async-done(((bf16[256,512]{1,0:T(8,128)(2,1)}), bf16[1024,512]{1,0:T(8,128)(2,1)}) %all-gather.4.cloned.1.call-update) | async-done | bytes 1048592 | tf_op jit(solution)/shard_map/all_gather | solution.py:66
  75.7 4.0 gather_fusion.1
  79.7 32.0 %all-gather.8.cloned.1.call-done = bf16[1024,2048]{1,0:T(8,128)(2,1)} async-done(((bf16[256,2048]{1,0:T(8,128)(2,1)}), bf16[1024,2048]{1,0:T(8,128)(2,1)}) %all-gather.8.cloned.1.call-update) | async-done | bytes 4194320 | tf_op jit(solution)/shard_map/all_gather | solution.py:67
  111.8 8.0 %gather_fusion.3 = bf16[512,2048]{1,0:T(8,128)(2,1)} fusion(bf16[1024,2048]{1,0:T(8,128)(2,1)} %all-gather.8.cloned.1.call-done, s32[1024]{0:T(1024)S(1)} %pad_clamp_fusion), kind=kCustom, calls=%fused_computation.3 | custom fusion | bytes 4196352 | tf_op jit(solution)/shard_map/jit(_take)/gather | solution.py:72
  119.7 3.7 abs_reduce_fusion
  123.5 9.9 %fusion.21 = f32[512,2048]{1,0:T(8,128)} fusion(bf16[2048,2048]{1,0:T(8,128)(2,1)} %param.6, bf16[512,2048]{1,0:T(8,128)(2,1)S(1)} %copy-done.4, pred[512]{0:T(512)(128)(4,1)S(1)} %compare_and_fusion.1), kind=kOutput, calls=%fused_computation.51 | convolution fusion | flops 4296015872 | bytes 14680576 | tf_op jit(solution)/shard_map/dot_general | solution.py:74
  133.3 1.3 copy.20
  134.6 2.1 fusion.17
  136.8 1.3 copy.21
  139.3 1.4 add_multiply_fusion
  141.8 11.7 %cholesky.103 = f32[128,128]{1,0:T(8,128)S(1)} custom-call(f32[128,128]{1,0:T(8,128)S(1)} %cholesky.263), custom_call_target="Cholesky" | custom-call | tf_op jit(solution)/shard_map/jit(cholesky)/cholesky | solution.py:52
  153.7 9.8 %custom-call.30 = f32[1,128,128]{1,2,0:T(8,128)S(1)} custom-call(f32[1,128,128]{2,1,0:T(8,128)S(1)} %get-tuple-element.37), custom_call_target="InvertDiagBlocksLowerTriangular" | custom-call | tf_op jit(solution)/shard_map/jit(cholesky)/cholesky | solution.py:52
  163.5 1.2 constant_dynamic-update-slice_fusion.3
  164.7 1.3 convolution_subtract_fusion.2
  166.0 11.7 %cholesky.215 = f32[128,128]{1,0:T(8,128)S(1)} custom-call(f32[128,128]{1,0:T(8,128)S(1)} %cholesky.267), custom_call_target="Cholesky" | custom-call | tf_op jit(solution)/shard_map/jit(cholesky)/cholesky | solution.py:52
  177.8 10.2 %custom-call.31 = f32[1,128,128]{1,2,0:T(8,128)S(1)} custom-call(f32[1,128,128]{2,1,0:T(8,128)S(1)} %get-tuple-element.34), custom_call_target="InvertDiagBlocksLowerTriangular" | custom-call | tf_op jit(solution)/shard_map/jit(cholesky)/cholesky | solution.py:52
  188.3 1.3 convolution_subtract_fusion.3
  189.6 11.7 %cholesky.236 = f32[128,128]{1,0:T(8,128)S(1)} custom-call(f32[128,128]{1,0:T(8,128)S(1)} %cholesky.272), custom_call_target="Cholesky" | custom-call | tf_op jit(solution)/shard_map/jit(cholesky)/cholesky | solution.py:52
  202.0 9.8 %custom-call.32 = f32[1,128,128]{1,2,0:T(8,128)S(1)} custom-call(f32[1,128,128]{2,1,0:T(8,128)S(1)} %get-tuple-element.31), custom_call_target="InvertDiagBlocksLowerTriangular" | custom-call | tf_op jit(solution)/shard_map/jit(cholesky)/cholesky | solution.py:52
  212.0 1.2 convolution_subtract_fusion.4
  213.2 11.8 %cholesky.253 = f32[128,128]{1,0:T(8,128)S(1)} custom-call(f32[128,128]{1,0:T(8,128)S(1)} %convolution_subtract_fusion.4), custom_call_target="Cholesky" | custom-call | tf_op jit(solution)/shard_map/jit(cholesky)/cholesky | solution.py:52
  228.8 1.1 select_select_fusion
  229.9 13.6 %while.1 = (s32[]{:T(128)}, f32[512,512]{1,0:T(8,128)}, s32[4,2]{0,1:T(2,128)S(1)}, f32[4,128,128]{2,1,0:T(8,128)}, s32[]{:T(128)}) while((s32[]{:T(128)}, f32[512,512]{1,0:T(8,128)}, s32[4,2]{0,1:T(2,128)S(1)}, f32[4,128,128]{2,1,0:T(8,128)}, s32[]{:T(128)}) %tuple.39), condition=%wide.while_cond, body=%wide.while_body.sunk | while | flops 2 | bytes 132705 | solution.py:77
  230.6 2.8 bitcast_dynamic-update-slice_fusion.2
  234.0 2.8 bitcast_dynamic-update-slice_fusion.2
  237.4 2.8 bitcast_dynamic-update-slice_fusion.2
  240.8 2.7 bitcast_dynamic-update-slice_fusion.2
  243.6 40.1 %custom-call.33 = f32[4,128,128]{1,2,0:T(8,128)S(1)} custom-call(f32[4,128,128]{2,1,0:T(8,128)} %get-tuple-element.9), custom_call_target="InvertDiagBlocksLowerTriangular" | custom-call | tf_op jit(solution)/shard_map/triangular_solve | solution.py:77
  283.7 3.7 exponential_subtract_fusion
  288.5 1.9 convolution_subtract_fusion.1
  291.4 2.2 convolution_subtract_fusion
  294.7 3.0 fusion.9
  297.7 1.1 convolution_convert_fusion
  299.4 1.3 copy-done
  301.7 1.7 pad_maximum_fusion
  303.5 116.1 %all-reduce.4.cloned.1.call-done = f32[2560,256]{1,0:T(8,128)} async-done(((f32[2560,256]{1,0:T(8,128)}), f32[2560,256]{1,0:T(8,128)}) %all-reduce.4.cloned.1.call-update) | async-done | bytes 2621456 | tf_op jit(solution)/shard_map/psum | solution.py:98
  420.5 5.1 %multiply_reduce_fusion = f32[2048]{0:T(1024)S(1)} fusion(bf16[2048,2048]{1,0:T(8,128)(2,1)} %param.6), kind=kLoop, calls=%fused_computation.6 | loop fusion | flops 12580864 | bytes 8396800 | tf_op jit(solution)/shard_map/reduce_sum | solution.py:93
  425.6 34.9 %psum.30 = f32[2560]{0:T(1024)S(1)} all-reduce(f32[2560]{0:T(1024)S(1)} %pad_maximum_fusion.2), channel_id=1, replica_groups=mesh['row'=4,'col'=8] {'col'}, use_global_device_ids=true, to_apply=%region_18.19 | all-reduce | flops 2560 | bytes 20480 | tf_op jit(solution)/shard_map/psum | solution.py:98
  460.6 11.8 %psum.31 = f32[2560]{0:T(1024)S(1)} all-reduce(f32[2560]{0:T(1024)S(1)} %psum.30), channel_id=1, replica_groups=mesh['row'=4,'col'=8] {'row'}, use_global_device_ids=true, to_apply=%region_19.20 | all-reduce | flops 2560 | bytes 20480 | tf_op jit(solution)/shard_map/psum | solution.py:98
  472.3 8.8 %all-reduce.6.cloned.1.call-done = f32[2560,256]{1,0:T(8,128)} async-done(((f32[2560,256]{1,0:T(8,128)}), f32[2560,256]{1,0:T(8,128)}) %all-reduce.6.cloned.1.call-update) | async-done | bytes 2621456 | tf_op jit(solution)/shard_map/psum | solution.py:98
  481.1 2.1 divide_convert_fusion
  483.3 5.9 %convolution_bitcast_fusion = f32[2048,256]{0,1:T(8,128)S(1)} fusion(bf16[2048,2048]{1,0:T(8,128)(2,1)} %param.6, bf16[2560,256]{1,0:T(8,128)(2,1)S(1)} %divide_convert_fusion), kind=kOutput, calls=%fused_computation.21 | convolution fusion | flops 2147483648 | bytes 11534336 | tf_op jit(solution)/shard_map/dot_general | solution.py:101
  490.0 1.8 copy.24
  (79 shorter events, 17.3 us)
Async XLA Ops:
  7.2 51.6 %all-gather.6.cloned.1.call-start = ((), (), s32[]{:S(2)}) async-start(), calls=%async_computation.1 | async-start | bytes 1179648 | tf_op jit(solution)/shard_map/all_gather | solution.py:63
  14.5 61.2 %all-gather.4.cloned.1.call-start = ((), (), s32[]{:S(2)}) async-start(), calls=%async_computation | async-start | bytes 1310720 | tf_op jit(solution)/shard_map/all_gather | solution.py:66
  14.6 2.3 copy-start.2
  16.8 42.1 %copy-start.8 = (s32[32]{0:T(128)S(1)}, s32[32]{0:T(128)}, u32[]{:S(2)}) copy-start(s32[32]{0:T(128)} %param.9) | copy-start | bytes 388
  16.9 42.7 %copy-start.6 = (bf16[2048,256]{1,0:T(8,128)(2,1)S(1)}, bf16[2048,256]{1,0:T(8,128)(2,1)}, u32[]{:S(2)}) copy-start(bf16[2048,256]{1,0:T(8,128)(2,1)} %param.7) | copy-start | bytes 3145732
  53.1 58.6 %all-gather.8.cloned.1.call-start = ((), (), s32[]{:S(2)}) async-start(), calls=%async_computation.2 | async-start | bytes 5242880 | tf_op jit(solution)/shard_map/all_gather | solution.py:67
  58.8 360.9 %all-reduce.4.cloned.1.call-start = ((), (), s32[]{:S(2)}) async-start(), calls=%async_computation.3 | async-start | bytes 5242880 | tf_op jit(solution)/shard_map/psum | solution.py:98
  119.7 3.8 copy-start.4
  140.8 1.0 copy-start.3
  297.7 3.0 copy-start.7
  299.4 1.3 copy-start
  299.4 2.3 copy-start.5
  303.4 177.6 %all-reduce.6.cloned.1.call-start = ((), (), s32[]{:S(2)}) async-start(), calls=%async_computation.4 | async-start | bytes 5242880 | tf_op jit(solution)/shard_map/psum | solution.py:98
  483.2 5.9 %copy-start.1 = (bf16[512,2048]{1,0:T(8,128)(2,1)S(1)}, bf16[512,2048]{1,0:T(8,128)(2,1)}, u32[]{:S(2)}) copy-start(bf16[512,2048]{1,0:T(8,128)(2,1)} %copy-done) | copy-start | bytes 6291460
Sparse Core Ops, SparseCore 0:
  14.7 44.0 all-gather.5
  60.3 15.3 all-gather.3
  77.3 34.4 all-gather.7
  303.6 116.0 all-reduce.3
  421.8 59.1 all-reduce.5
